TPU v7x, 32 devices: a whole 2x2x4 slice. The times are simulated.
32 devices in a mesh: pipe: 2 (over x), expert: 16 (over z, y, core).
Axes of the slice: x: 2, y: 2, z: 4, core: 2. Of those that a mesh axis runs over, the one named last changes fastest.
Arguments:
- inputs: bfloat16 [1, 512, 5120], P(None, 'expert'), may hold values from -6 to 6
- router: bfloat16 [2, 5120, 2], P('pipe'), may hold values from -0.078125 to 0.078125
- w_up: bfloat16 [2, 3072, 5120], P('pipe', 'expert'), may hold values from -0.078125 to 0.078125
- w_down: bfloat16 [2, 3072, 5120], P('pipe', 'expert'), may hold values from -0.15625 to 0.15625
- picks: int32 [2, 1, 2, 8], P('pipe'), may hold values from 0 to 511, as said below
- probe: bfloat16 [2, 64, 5120], P('pipe'), may hold values from -0.078125 to 0.078125
Outputs:
- student_feats: bfloat16 [2, 1, 512, 64], P('pipe', None, 'expert')
Inputs may be any that keep to these rules, and one draw needn't show every extreme that they name: Each list picks[s, m, e] holds 8 different token positions of the micro-batch. Of the 32 consecutive positions held by one index of expert, at most 1 stand in one list, and in every list some index has exactly 1.
All inputs are finite; a program needn't handle non-finite values.
Results may differ from a plain program's by a relative error of at most 0.0059.
Values may be sent and summed in bfloat16 or wider, within the bound.
A program may use at most 64 MiB of HBM per device.

v0:
```python
import functools

import jax
import jax.numpy as jnp
from jax import lax
from jax.experimental import pallas as pl
from jax.experimental.pallas import tpu as pltpu
from jax.sharding import PartitionSpec as P

EPS = 1e-06
CUT = 8
PAD = 16
JOIN = 2
MESH = pl.DeviceIdType.MESH
NT = (((1,), (1,)), ((), ()))


def kernel(
    sections, width, experts, x_hbm, router_hbm, up_hbm, down_hbm, picks_hbm, probe_hbm, out_ref,
    x_ref, up_ref, down_ref, probe_ref, scorer, lists, place, rows, picked, arrived, stage,
    partial, returned, state_out, state_in, load_sem, list_send, list_recv, row_send, row_recv,
    part_send, part_recv, state_send, state_recv,
):
    section = lax.axis_index("pipe")
    me = lax.axis_index("expert")
    tokens, features = x_ref.shape
    hidden_units = up_hbm.shape[0]
    piece = features // CUT
    group = width // experts
    slots = sections * experts
    expert = me // group
    barrier = pltpu.get_barrier_semaphore()

    def around(step):
        index = me + step
        return jnp.where(index >= width, index - width, index)

    def far_pipe(far):
        index = section + far
        return jnp.where(index >= sections, index - sections, index)

    def expert_of(index):
        owner = jnp.int32(0)
        for e in range(1, experts):
            owner = owner + (index >= e * group).astype(jnp.int32)
        return owner

    steps = range(1, width)

    def each_step(act):
        if width <= 16:
            for step in steps:
                act(step)
        else:
            lax.fori_loop(1, width, lambda step, carry: (act(step), carry)[1], 0)

    def greet(step):
        other = around(step)
        for far in range(sections):
            to = far_pipe(far)
            pl.semaphore_signal(barrier, inc=1, device_id=(to, other), device_id_type=MESH)

    for far in range(1, sections):
        to = far_pipe(far)
        pl.semaphore_signal(barrier, inc=1, device_id=(to, me), device_id_type=MESH)
    each_step(greet)

    loads = [
        pltpu.make_async_copy(picks_hbm, lists.at[section], load_sem.at[0]),
        pltpu.make_async_copy(x_hbm, x_ref, load_sem.at[1]),
        pltpu.make_async_copy(up_hbm, up_ref.at[pl.ds(0, hidden_units)], load_sem.at[2]),
        pltpu.make_async_copy(router_hbm, scorer, load_sem.at[3]),
        pltpu.make_async_copy(down_hbm, down_ref, load_sem.at[4]),
        pltpu.make_async_copy(probe_hbm, probe_ref, load_sem.at[5]),
    ]
    for load in loads:
        load.start()
    loads[0].wait()
    loads[1].wait()

    def places_of(section_lists):
        wide = jnp.concatenate(
            [jnp.broadcast_to(section_lists[e : e + 1], (CUT, section_lists.shape[1]))
             for e in range(experts)], axis=0,
        )
        local = wide - me * tokens
        owned = (local >= 0) & (local < tokens)
        found = jnp.where(owned, local + 1, 0).astype(jnp.float32)
        return jnp.sum(found, axis=1, keepdims=True) - 1.0

    def select(places):
        height = experts * CUT
        token_id = lax.broadcasted_iota(jnp.int32, (height, tokens), 1).astype(jnp.float32)
        cut_id = lax.rem(lax.broadcasted_iota(jnp.int32, (height, tokens), 0), CUT)
        hot = places == token_id
        total = jnp.zeros((height, piece), jnp.float32)
        for c in range(CUT):
            pick = jnp.where(hot & (cut_id == c), 1.0, 0.0).astype(jnp.bfloat16)
            total += jnp.dot(
                pick, x_ref[:, c * piece : (c + 1) * piece], preferred_element_type=jnp.float32
            )
        return total

    def note(which):
        places = places_of(lists[which])
        chosen = select(places)
        first = which * experts
        place[pl.ds(first, experts)] = jnp.broadcast_to(
            places, (experts * CUT, piece)
        ).reshape(experts, CUT, piece)
        rows[pl.ds(first, experts)] = chosen.reshape(experts, CUT, piece)

    note(section)

    def send_rows():
        picked[...] = rows[pl.ds(section * experts, experts)].astype(jnp.bfloat16)

        def send(step):
            other = around(step)
            pltpu.make_async_remote_copy(
                src_ref=picked.at[expert_of(other)], dst_ref=arrived.at[me], send_sem=row_send,
                recv_sem=row_recv, device_id=(section, other), device_id_type=MESH,
            ).start()

        each_step(send)
        pltpu.make_async_copy(picked.at[expert], arrived.at[me], row_recv).start()

    pl.semaphore_wait(barrier, sections * width - 1)

    @pl.when(section == 0)
    def _():
        send_rows()

    def list_copy(far):
        to = far_pipe(far)
        return pltpu.make_async_remote_copy(
            src_ref=lists.at[section], dst_ref=lists.at[section], send_sem=list_send.at[far],
            recv_sem=list_recv.at[far], device_id=(to, me), device_id_type=MESH,
        )

    for far in range(1, sections):
        list_copy(far).start()

    loads[5].wait()
    x_all = x_ref[...]
    raw = lax.dot_general(x_all, probe_ref[...], NT, preferred_element_type=jnp.float32)
    x_wide = x_all.astype(jnp.float32)
    square = jnp.sum(x_wide * x_wide, axis=1, keepdims=True)
    base = raw * lax.rsqrt(square * (1.0 / features) + EPS)

    for far in range(1, sections):
        list_copy(far).wait()
        note(lax.rem(section + sections - far, sections))

    loads[2].wait()
    loads[3].wait()
    up_ref[pl.ds(hidden_units, PAD)] = jnp.zeros((PAD, features), jnp.bfloat16)
    up_ref[pl.ds(hidden_units, experts)] = scorer[...]
    loads[4].wait()

    def over_cuts(value):
        count, lanes = value.shape
        summed = jnp.sum(value.reshape(count // CUT, CUT, lanes), axis=1, keepdims=True)
        return jnp.broadcast_to(summed, (count // CUT, CUT, lanes)).reshape(count, lanes)

    def expert_block():
        wide = arrived[...].astype(jnp.float32).reshape(width * CUT, piece)
        lanes = stage.shape[2]
        for t in range(piece // lanes):
            stage[t] = wide[:, t * lanes : (t + 1) * lanes]
        squares = jnp.sum((wide * wide).reshape(width, CUT, piece), axis=1)
        scale = lax.rsqrt(jnp.sum(squares, axis=1, keepdims=True) * (1.0 / features) + EPS)
        columns = up_ref.shape[0]
        pre = jnp.zeros((width, columns), jnp.float32)
        for c in range(0, CUT, JOIN):
            pre += lax.dot_general(
                jnp.concatenate(
                    [stage[t, pl.ds(c + i, width, stride=CUT)]
                     for i in range(JOIN) for t in range(piece // lanes)], axis=1
                ).astype(jnp.bfloat16),
                up_ref[:, c * piece : (c + JOIN) * piece], NT,
                preferred_element_type=jnp.float32,
            )
        pre = pre * scale
        column = lax.broadcasted_iota(jnp.int32, (width, columns), 1)
        logit = jnp.sum(
            jnp.where(column == hidden_units + expert, pre, 0.0), axis=1, keepdims=True
        )
        value = pre[:, :hidden_units]
        gate = 1.0 / (1.0 + jnp.exp(-logit))
        hidden = (value / (1.0 + jnp.exp(-value)) * gate).astype(jnp.bfloat16)
        for c in range(0, CUT, JOIN):
            block = jnp.dot(
                hidden, down_ref[:, c * piece : (c + JOIN) * piece],
                preferred_element_type=jnp.float32,
            )
            for i in range(JOIN):
                for t in range(piece // lanes):
                    at = i * piece + t * lanes
                    stage[t, pl.ds(c + i, width, stride=CUT)] = block[:, at : at + lanes]
        for t in range(piece // lanes):
            partial[:, :, t * lanes : (t + 1) * lanes] = (
                stage[t].reshape(width, CUT, lanes).astype(jnp.bfloat16)
            )

    def give(owner, far, batch):
        pltpu.make_async_remote_copy(
            src_ref=partial.at[owner], dst_ref=returned.at[batch, me],
            send_sem=part_send.at[far], recv_sem=part_recv.at[batch],
            device_id=(far_pipe(far), owner), device_id_type=MESH,
        ).start()

    def pass_parts():
        each_step(lambda step: give(around(step), 1, 0))
        give(me, 1, 0)

    def share_parts():
        for far in reversed(range(1, sections)):
            give(me, far, 1)
            each_step(lambda step: give(around(step), far, 1))
        each_step(lambda step: give(around(step), 0, 1))
        pltpu.make_async_copy(partial.at[me], returned.at[1, me], part_recv.at[1]).start()

    def give_state(far, batch):
        return pltpu.make_async_remote_copy(
            src_ref=state_out, dst_ref=state_in.at[batch], send_sem=state_send.at[far],
            recv_sem=state_recv.at[batch], device_id=(far_pipe(far), me), device_id_type=MESH,
        )

    def take_state(batch):
        pltpu.make_async_copy(state_in.at[batch], state_in.at[batch], state_recv.at[batch]).wait()
        rows[...] = state_in[batch].astype(jnp.float32)

    def take_parts(phase, batch):
        pltpu.make_async_copy(returned.at[batch], returned.at[batch], part_recv.at[batch]).wait()
        updates = [
            jnp.sum(returned[batch, pl.ds(e * group, group)].astype(jnp.float32), axis=0)
            for e in range(experts)
        ]

        def apply(slot, carry):
            total = jnp.zeros((CUT, piece), jnp.float32)
            for e in range(experts):
                same = place[slot] == place[phase * experts + e]
                total += jnp.where(same, updates[e], 0.0)
            rows[slot] = (rows[slot] + total).astype(jnp.bfloat16).astype(jnp.float32)
            return carry

        lax.fori_loop(0, slots, apply, 0, unroll=slots <= 8)

    last = sections - 1

    @pl.when(section < last)
    def _():
        @pl.when(section > 0)
        def _():
            @pl.when(section > 1)
            def _():
                take_state(0)

            take_parts(section - 1, 0)
            send_rows()
            state_out[...] = rows[...].astype(jnp.bfloat16)
            give_state(1, 0).start()

        pltpu.make_async_copy(arrived, arrived, row_recv).wait()
        expert_block()
        pass_parts()

    @pl.when(section == last)
    def _():
        if last > 0:
            if last > 1:
                take_state(0)
            take_parts(section - 1, 0)
            send_rows()
            state_out[...] = rows[...].astype(jnp.bfloat16)
            for far in range(1, sections):
                give_state(far, 1).start()
        pltpu.make_async_copy(arrived, arrived, row_recv).wait()
        expert_block()
        share_parts()

    if last > 0:
        @pl.when(section < last)
        def _():
            take_state(1)

    take_parts(last, 1)

    height = slots * CUT
    wide = rows[...].reshape(height, piece)
    mean = over_cuts(jnp.sum(wide * wide, axis=1, keepdims=True)) * (1.0 / features)
    narrow = wide.astype(jnp.bfloat16)
    feats = probe_ref.shape[0]
    cut_out = lax.rem(lax.broadcasted_iota(jnp.int32, (height, feats), 0), CUT)
    changed = jnp.zeros((height, feats), jnp.float32)
    for c in range(CUT):
        term = lax.dot_general(
            narrow, probe_ref[:, c * piece : (c + 1) * piece], NT,
            preferred_element_type=jnp.float32,
        )
        changed = jnp.where(cut_out == c, term, changed)
    changed = over_cuts(changed) * lax.rsqrt(mean + EPS)
    token_id = lax.broadcasted_iota(jnp.int32, (tokens, feats), 0).astype(jnp.float32)
    result = base
    for slot in range(slots):
        at = place[slot][:1, :feats]
        result = jnp.where(token_id == at, changed[slot * CUT : slot * CUT + 1], result)
    out_ref[...] = result.astype(out_ref.dtype)

    most = returned.at[0, pl.ds(0, width - 1)]
    pltpu.make_async_copy(most, most, row_send).wait()

    @pl.when(section < last)
    def _():
        pltpu.make_async_copy(returned.at[0], returned.at[0], part_send.at[1 % sections]).wait()

        @pl.when(section > 0)
        def _():
            give_state(1, 0).wait_send()

    @pl.when(section == last)
    def _():
        pltpu.make_async_copy(most, most, part_send.at[0]).wait()
        for far in range(1, sections):
            pltpu.make_async_copy(returned.at[0], returned.at[0], part_send.at[far]).wait()
            give_state(far, 1).wait_send()


def shards(inputs, router, w_up, w_down, picks, probe):
    sections = lax.axis_size("pipe")
    width = lax.axis_size("expert")
    tokens, features = inputs.shape[1:]
    experts = router.shape[2]
    cap = picks.shape[3]
    hidden_units = w_up.shape[1]
    feats = probe.shape[1]
    piece = features // CUT
    slots = sections * experts
    any_spec = pl.BlockSpec(memory_space=pl.ANY)
    out = pl.pallas_call(
        functools.partial(kernel, sections, width, experts),
        out_shape=jax.ShapeDtypeStruct((tokens, feats), jnp.bfloat16),
        in_specs=[any_spec] * 6,
        out_specs=pl.BlockSpec(memory_space=pltpu.VMEM),
        scratch_shapes=[
            pltpu.VMEM((tokens, features), jnp.bfloat16),
            pltpu.VMEM((hidden_units + PAD, features), jnp.bfloat16),
            pltpu.VMEM((hidden_units, features), jnp.bfloat16),
            pltpu.VMEM((feats, features), jnp.bfloat16),
            pltpu.VMEM((experts, features), jnp.bfloat16),
            pltpu.VMEM((sections, experts, cap), jnp.int32),
            pltpu.VMEM((slots, CUT, piece), jnp.float32),
            pltpu.VMEM((slots, CUT, piece), jnp.float32),
            pltpu.VMEM((experts, CUT, piece), jnp.bfloat16),
            pltpu.VMEM((width, CUT, piece), jnp.bfloat16),
            pltpu.VMEM((piece // 128, width * CUT, 128), jnp.float32),
            pltpu.VMEM((width, CUT, piece), jnp.bfloat16),
            pltpu.VMEM((2, width, CUT, piece), jnp.bfloat16),
            pltpu.VMEM((slots, CUT, piece), jnp.bfloat16),
            pltpu.VMEM((2, slots, CUT, piece), jnp.bfloat16),
            pltpu.SemaphoreType.DMA((6,)),
            pltpu.SemaphoreType.DMA((sections,)),
            pltpu.SemaphoreType.DMA((sections,)),
            pltpu.SemaphoreType.DMA,
            pltpu.SemaphoreType.DMA,
            pltpu.SemaphoreType.DMA((sections,)),
            pltpu.SemaphoreType.DMA((2,)),
            pltpu.SemaphoreType.DMA((sections,)),
            pltpu.SemaphoreType.DMA((2,)),
        ],
        compiler_params=pltpu.CompilerParams(collective_id=0, has_side_effects=True),
        name="relay",
    )(inputs[0], jnp.transpose(router[0]), w_up[0], w_down[0], picks[0, 0], probe[0])
    return out[None, None]


def solution(mesh):
    return jax.shard_map(
        shards,
        mesh=mesh,
        in_specs=(
            P(None, "expert", None),
            P("pipe", None, None),
            P("pipe", "expert", None),
            P("pipe", "expert", None),
            P("pipe", None, None, None),
            P("pipe", None, None),
        ),
        out_specs=P("pipe", None, "expert", None),
        check_vma=False,
    )
```

profile of v0, /device:TPU:3, one launch (start us, length us, event | category | flops | bytes accessed | tf_op | source)
XLA Modules:
  0.0 36.6 jit_solution(346806260566161726)
XLA Ops:
  0.0 35.3 %relay.1 = bf16[32,64]{1,0:T(8,128)(2,1)} custom-call(bf16[32,5120]{1,0:T(8,128)(2,1)} %bitcast.12, bf16[2,5120]{1,0:T(2,128)(2,1)} %bitcast.14, bf16[192,5120]{1,0:T(8,128)(2,1)} %bitcast.9, bf16[192,5120]{1,0:T(8,128)(2,1)} %bitcast.10, s32[2,8]{1,0:T(2,128)} %bitcast.15, bf16[64,5120]{1,0:T(8,128)(2,1)} %bitcast.11), custom_call_target="tpu_custom_call" | custom-call | tf_op jit(solution)/shard_map/relay/pallas_call | solution.py:342
  35.3 1.3 %copy.8 = bf16[1,1,32,64]{3,2,1,0:T(8,128)(2,1)} copy(bf16[1,1,32,64]{3,2,1,0:T(8,128)(2,1)} %bitcast.13) | data formatting | bytes 8192
where the time goes:
time: 36.8 us; the launch traced here: 36.6 us
  Pallas kernels  35.3 us (96%)
  local copies, waits for them, and re-layouts  1.3 us (4%)
    pallas_call x1, Pallas kernels, shards(): pl.pallas_call(functools.partial(kernel, sections, width, experts), out_s...  35.3 us
    unnamed x1, local copies, waits for them, and re-layouts  1.3 us

commit v1 on v0

v1 whole, which is shorter than its diff:
```python
import functools

import jax
import jax.numpy as jnp
from jax import lax
from jax.experimental import pallas as pl
from jax.experimental.pallas import tpu as pltpu
from jax.sharding import PartitionSpec as P

EPS = 1e-06
CUT = 8
PAD = 16
JOIN = 2
LANE = 128
BLOCK = 8
MESH = pl.DeviceIdType.MESH
NT = (((1,), (1,)), ((), ()))


class Plan:
    def __init__(self, sections, width, features):
        self.piece = features // CUT
        tiles = self.piece // LANE
        self.per = width // CUT
        self.parts = min(self.per, tiles, sections)
        sizes = [tiles // self.parts + (q < tiles % self.parts) for q in range(self.parts)]
        starts = [sum(sizes[:q]) for q in range(self.parts)]
        self.window = max(sizes) * LANE
        self.size = [size * LANE for size in sizes]
        self.start = [start * LANE for start in starts]
        self.win = [min(start, self.piece - self.window) for start in self.start]
        self.off = [start - win for start, win in zip(self.start, self.win)]


def kernel(
    sections, width, experts, plan, x_hbm, router_hbm, up_hbm, down_hbm, picks_hbm, probe_hbm,
    out_ref, x_ref, up_ref, down_ref, probe_ref, scorer, lists, columns, place, picked, arrived,
    stage, listed, xrows, xin, base_rows, pin, state_out, state_in, sent, fed, owed, owing, held,
    partial, returned, done_out, done_in, load_sem, list_send, list_recv, row_send, row_recv,
    x_send, x_recv, pin_send, pin_recv, state_send, state_recv, fed_send, fed_recv, owe_send,
    owe_recv, part_send, part_recv, done_send, done_recv,
):
    section = lax.axis_index("pipe")
    me = lax.axis_index("expert")
    tokens, features = x_ref.shape
    hidden_units = up_hbm.shape[0]
    cap = lists.shape[2]
    piece, per, parts, window = plan.piece, plan.per, plan.parts, plan.window
    group = width // experts
    slots = sections * experts
    blocks, filled = xin.shape[1], min(slots, BLOCK)
    last = sections - 1
    expert = me // group
    my_cut = me // per
    my_part = lax.rem(me, per)
    barrier = pltpu.get_barrier_semaphore()

    def far_pipe(far):
        index = section + far
        return jnp.where(index >= sections, index - sections, index)

    def each_other(act):
        if width <= 16:
            for step in reversed(range(1, width)):
                act(jnp.bitwise_xor(me, step))
        else:
            lax.fori_loop(
                1, width, lambda step, carry: (act(jnp.bitwise_xor(me, width - step)), carry)[1], 0
            )

    def if_slicing(act):
        if per == parts:
            act()
        else:
            pl.when(my_part < parts)(act)

    def remote(src, dst, send, recv, to):
        return pltpu.make_async_remote_copy(
            src_ref=src, dst_ref=dst, send_sem=send, recv_sem=recv, device_id=to,
            device_id_type=MESH,
        )

    def wait(ref, sem):
        pltpu.make_async_copy(ref, ref, sem).wait()

    def greet(other):
        for far in range(sections):
            pl.semaphore_signal(
                barrier, inc=1, device_id=(far_pipe(far), other), device_id_type=MESH
            )

    for far in range(1, sections):
        pl.semaphore_signal(barrier, inc=1, device_id=(far_pipe(far), me), device_id_type=MESH)
    each_other(greet)

    loads = [
        pltpu.make_async_copy(picks_hbm, lists.at[section], load_sem.at[0]),
        pltpu.make_async_copy(x_hbm, x_ref, load_sem.at[1]),
        pltpu.make_async_copy(up_hbm, up_ref.at[pl.ds(0, hidden_units)], load_sem.at[2]),
        pltpu.make_async_copy(router_hbm, scorer, load_sem.at[3]),
        pltpu.make_async_copy(down_hbm, down_ref, load_sem.at[4]),
        pltpu.make_async_copy(probe_hbm, probe_ref, load_sem.at[5]),
    ]
    for load in loads:
        load.start()
    loads[0].wait()
    loads[1].wait()

    def places_of(section_lists):
        wide = jnp.concatenate(
            [jnp.broadcast_to(section_lists[e : e + 1], (CUT, section_lists.shape[1]))
             for e in range(experts)], axis=0,
        )
        local = wide - me * tokens
        owned = (local >= 0) & (local < tokens)
        found = jnp.where(owned, local + 1, 0).astype(jnp.float32)
        return jnp.sum(found, axis=1, keepdims=True) - 1.0

    def select(places):
        height = experts * CUT
        token_id = lax.broadcasted_iota(jnp.int32, (height, tokens), 1).astype(jnp.float32)
        cut_id = lax.rem(lax.broadcasted_iota(jnp.int32, (height, tokens), 0), CUT)
        hot = places == token_id
        total = jnp.zeros((height, piece), jnp.float32)
        for c in range(CUT):
            pick = jnp.where(hot & (cut_id == c), 1.0, 0.0).astype(jnp.bfloat16)
            total += jnp.dot(
                pick, x_ref[:, c * piece : (c + 1) * piece], preferred_element_type=jnp.float32
            )
        return total

    def note(which):
        section_lists = lists[which]
        places = places_of(section_lists)
        place[pl.ds(which * experts, experts)] = jnp.broadcast_to(
            places, (experts * CUT, LANE)
        ).reshape(experts, CUT, LANE)
        diagonal = lax.broadcasted_iota(jnp.int32, (cap, cap), 0) == lax.broadcasted_iota(
            jnp.int32, (cap, cap), 1
        )
        for e in range(experts):
            wide = jnp.broadcast_to(section_lists[e : e + 1], (cap, cap)).astype(jnp.float32)
            column = jnp.sum(jnp.where(diagonal, wide, 0.0), axis=1, keepdims=True)
            columns[which * experts + e] = jnp.broadcast_to(column, columns.shape[1:])
        return places

    places = note(section)

    @pl.when(section == 0)
    def _():
        picked[...] = select(places).astype(jnp.bfloat16).reshape(experts, CUT, piece)

    pl.semaphore_wait(barrier, sections * width - 1)

    def expert_of(index):
        owner = jnp.int32(0)
        for e in range(1, experts):
            owner = owner + (index >= e * group).astype(jnp.int32)
        return owner

    @pl.when(section == 0)
    def _():
        each_other(
            lambda other: remote(
                picked.at[expert_of(other)], arrived.at[me], row_send, row_recv, (section, other)
            ).start()
        )
        pltpu.make_async_copy(picked.at[expert], arrived.at[me], row_recv).start()

    def list_copy(far):
        return remote(
            lists.at[section], lists.at[section], list_send.at[far], list_recv.at[far],
            (far_pipe(far), me),
        )

    for far in range(1, sections):
        list_copy(far).start()
    for far in range(1, sections):
        list_copy(far).wait()
        note(lax.rem(section + sections - far, sections))

    def each_slice(act):
        for step in reversed(range(CUT)):
            cut = jnp.bitwise_xor(my_cut, step)
            for q in range(parts):
                act(step, cut, q, cut * per + q)

    def owner_lanes(height_rows, first_block):
        rows_n, lanes_n = filled * cap, width * BLOCK
        row_slot = lax.broadcasted_iota(jnp.int32, (rows_n, lanes_n), 0) // cap
        lane = lax.broadcasted_iota(jnp.int32, (rows_n, lanes_n), 1)
        low = (lane // BLOCK * tokens).astype(jnp.float32)
        return (row_slot == lane % BLOCK) & (height_rows >= low) & (height_rows < low + tokens)

    def column_of(block):
        wide = columns[pl.ds(block * filled, filled)]
        return wide.reshape(filled * cap, wide.shape[2])[:, :1]

    def row_of(column):
        count = column.shape[0]
        diagonal = lax.broadcasted_iota(jnp.int32, (count, count), 0) == lax.broadcasted_iota(
            jnp.int32, (count, count), 1
        )
        wide = jnp.where(diagonal, jnp.broadcast_to(column, (count, count)), 0.0)
        return jnp.sum(wide, axis=0, keepdims=True)

    @pl.when(section == 1)
    def _():
        token_id = lax.broadcasted_iota(jnp.int32, (BLOCK, tokens), 1).astype(jnp.float32)
        row_id = lax.broadcasted_iota(jnp.int32, (BLOCK, tokens), 0)
        for b in range(blocks):
            hot = jnp.zeros((BLOCK, tokens), jnp.float32)
            for i in range(filled):
                at = place[b * filled + i][:1, :1]
                hot = jnp.where((row_id == i) & (at == token_id), 1.0, hot)
            for c in range(CUT):
                xrows[c, b] = jnp.dot(
                    hot.astype(jnp.bfloat16), x_ref[:, c * piece : (c + 1) * piece],
                    preferred_element_type=jnp.float32,
                ).astype(jnp.bfloat16)

        def send(step, cut, q, device):
            src = xrows.at[cut, :, :, pl.ds(plan.win[q], window)]

            def away():
                remote(src, xin.at[me], x_send, x_recv, (section, device)).start()

            if step:
                away()
            else:
                pl.when(device != me)(away)

                @pl.when(device == me)
                def _():
                    pltpu.make_async_copy(src, xin.at[me], x_recv).start()

        each_slice(send)

    loads[5].wait()
    x_all = x_ref[...]
    raw = lax.dot_general(x_all, probe_ref[...], NT, preferred_element_type=jnp.float32)
    x_wide = x_all.astype(jnp.float32)
    square = jnp.sum(x_wide * x_wide, axis=1, keepdims=True)
    base = raw * lax.rsqrt(square * (1.0 / features) + EPS)

    loads[2].wait()
    loads[3].wait()
    up_ref[pl.ds(hidden_units, PAD)] = jnp.zeros((PAD, features), jnp.bfloat16)
    up_ref[pl.ds(hidden_units, experts)] = scorer[...]
    loads[4].wait()

    @pl.when(section == 1)
    def _():
        def gather():
            wait(xin, x_recv)
            for b in range(blocks):
                rows = xin[:, b].astype(jnp.float32).reshape(width * BLOCK, window)
                hot = owner_lanes(column_of(b), b).astype(jnp.float32).astype(jnp.bfloat16)
                total = jnp.dot(hot, rows.astype(jnp.bfloat16), preferred_element_type=jnp.float32)
                base_rows[pl.ds(b * filled, filled)] = total.reshape(filled, cap, window)

        if_slicing(gather)

    def hidden_of(pre, squares):
        scale = lax.rsqrt(squares * (1.0 / features) + EPS)
        pre = pre * scale
        column = lax.broadcasted_iota(jnp.int32, pre.shape, 1)
        logit = jnp.sum(
            jnp.where(column == hidden_units + expert, pre, 0.0), axis=1, keepdims=True
        )
        value = pre[:, :hidden_units]
        gate = 1.0 / (1.0 + jnp.exp(-logit))
        return (value / (1.0 + jnp.exp(-value)) * gate).astype(jnp.bfloat16)

    def first_hidden():
        wait(arrived, row_recv)
        wide = arrived[...].astype(jnp.float32).reshape(width * CUT, piece)
        for t in range(piece // LANE):
            stage[t] = wide[:, t * LANE : (t + 1) * LANE]
        squares = jnp.sum((wide * wide).reshape(width, CUT, piece), axis=1)
        pre = jnp.zeros((width, up_ref.shape[0]), jnp.float32)
        for c in range(0, CUT, JOIN):
            pre += lax.dot_general(
                jnp.concatenate(
                    [stage[t, pl.ds(c + i, width, stride=CUT)]
                     for i in range(JOIN) for t in range(piece // LANE)], axis=1
                ).astype(jnp.bfloat16),
                up_ref[:, c * piece : (c + JOIN) * piece], NT,
                preferred_element_type=jnp.float32,
            )
        hidden = hidden_of(pre, jnp.sum(squares, axis=1, keepdims=True))
        column = columns[section * experts + expert][:, :1]
        low = (lax.broadcasted_iota(jnp.int32, (cap, width), 1) * tokens).astype(jnp.float32)
        hot = jnp.where((column >= low) & (column < low + tokens), 1.0, 0.0).astype(jnp.bfloat16)
        return jnp.dot(hot, hidden, preferred_element_type=jnp.float32).astype(jnp.bfloat16)

    def next_hidden():
        pre = jnp.zeros((cap, up_ref.shape[0]), jnp.float32)
        squares = jnp.zeros((cap, piece), jnp.float32)
        for step in range(CUT):
            cut = jnp.bitwise_xor(my_cut, step)
            for q in range(parts):
                wait(fed.at[cut * per + q], fed_recv.at[cut * per + q])
            chunk = jnp.concatenate(
                [fed[cut * per + q][:, plan.off[q] : plan.off[q] + plan.size[q]]
                 for q in range(parts)], axis=1,
            )
            wide = chunk.astype(jnp.float32)
            squares += wide * wide
            pre += lax.dot_general(
                chunk, up_ref[:, pl.ds(pl.multiple_of(cut * piece, LANE), piece)], NT,
                preferred_element_type=jnp.float32,
            )
        return hidden_of(pre, jnp.sum(squares, axis=1, keepdims=True))

    def pass_lists(hidden):
        def send(step, cut, q, device):
            if q == 0:
                listed[cut] = jnp.dot(
                    hidden, down_ref[:, pl.ds(pl.multiple_of(cut * piece, LANE), piece)],
                    preferred_element_type=jnp.float32,
                ).astype(jnp.bfloat16)
            remote(
                listed.at[cut, :, pl.ds(plan.win[q], window)], pin.at[me], pin_send, pin_recv,
                (section + 1, device),
            ).start()

        each_slice(send)

    def share_parts(hidden):
        own_list = jnp.zeros((1, cap), jnp.int32)
        for e in range(experts):
            own_list = jnp.where(expert == e, lists[section][e : e + 1], own_list)
        low = lax.broadcasted_iota(jnp.int32, (width, cap), 0) * tokens
        hot = (own_list >= low) & (own_list < low + tokens)
        hidden = jnp.dot(
            jnp.where(hot, 1.0, 0.0).astype(jnp.bfloat16), hidden,
            preferred_element_type=jnp.float32,
        ).astype(jnp.bfloat16)
        for c in range(0, CUT, JOIN):
            block = jnp.dot(
                hidden, down_ref[:, c * piece : (c + JOIN) * piece],
                preferred_element_type=jnp.float32,
            )
            for i in range(JOIN):
                for t in range(piece // LANE):
                    at = i * piece + t * LANE
                    stage[t, pl.ds(c + i, width, stride=CUT)] = block[:, at : at + LANE]
        for t in range(piece // LANE):
            partial[:, :, t * LANE : (t + 1) * LANE] = (
                stage[t].reshape(width, CUT, LANE).astype(jnp.bfloat16)
            )

        def refs(owner, q):
            return (
                partial.at[owner, :, pl.ds(plan.start[q], plan.size[q])],
                returned.at[me, :, pl.ds(plan.off[q], plan.size[q])],
            )

        def give(owner, q):
            src, dst = refs(owner, q)
            remote(src, dst, part_send.at[q], part_recv, (section - q, owner)).start()

        for q in reversed(range(1, parts)):
            give(me, q)

        def give_all(owner):
            for q in reversed(range(parts)):
                give(owner, q)

        each_other(give_all)
        src, dst = refs(me, 0)
        pltpu.make_async_copy(src, dst, part_recv).start()

    def state_copy():
        return remote(state_out, state_in, state_send, state_recv, (section + 1, me))

    def take_lists(last_section):
        if sections > 2:
            @pl.when(section > 1)
            def _():
                wait(state_in, state_recv)
                base_rows[...] = state_in[...].astype(jnp.float32)

        wait(pin, pin_recv)
        sums = jnp.concatenate(
            [jnp.sum(pin[pl.ds(e * group, group)].astype(jnp.float32), axis=0)
             for e in range(experts)], axis=0,
        )
        high = sums.astype(jnp.bfloat16)
        low = (sums - high.astype(jnp.float32)).astype(jnp.bfloat16)
        before = columns[pl.ds((section - 1) * experts, experts)]
        entries = row_of(before.reshape(experts * cap, before.shape[2])[:, :1])

        def grow(first, count):
            wide = columns[pl.ds(first, count)]
            same = wide.reshape(count * cap, wide.shape[2])[:, :1] == entries
            hot = jnp.where(same, 1.0, 0.0).astype(jnp.bfloat16)
            added = jnp.dot(hot, high, preferred_element_type=jnp.float32) + jnp.dot(
                hot, low, preferred_element_type=jnp.float32
            )
            rows = base_rows[pl.ds(first, count)] + added.reshape(count, cap, window)
            return rows.astype(jnp.bfloat16)

        sent[...] = grow(section * experts, experts)
        each_other(
            lambda other: remote(
                sent.at[expert_of(other)], fed.at[me], fed_send, fed_recv.at[me], (section, other)
            ).start()
        )
        pltpu.make_async_copy(sent.at[expert], fed.at[me], fed_recv.at[me]).start()
        for b in range(blocks):
            rows = grow(b * filled, filled)
            if sections > 2:
                state_out[pl.ds(b * filled, filled)] = rows
            owed_block(b, rows.reshape(filled * cap, window))
        if sections > 2:
            pl.when(section < last)(lambda: state_copy().start())
        pl.when(section == last)(owe)

    def owed_block(b, rows):
        @pl.when(section == last)
        def _():
            rows_n, lanes_n = width * BLOCK, filled * cap
            entry = row_of(column_of(b))
            row = lax.broadcasted_iota(jnp.int32, (rows_n, lanes_n), 0)
            lane_slot = lax.broadcasted_iota(jnp.int32, (rows_n, lanes_n), 1) // cap
            low = (row // BLOCK * tokens).astype(jnp.float32)
            hot = (row % BLOCK == lane_slot) & (entry >= low) & (entry < low + tokens)
            total = jnp.dot(
                jnp.where(hot, 1.0, 0.0).astype(jnp.bfloat16), rows,
                preferred_element_type=jnp.float32,
            )
            owed[:, b] = total.reshape(width, BLOCK, window).astype(jnp.bfloat16)

    def owe():
        def send(owner):
            remote(
                owed.at[owner], owing.at[my_cut], owe_send, owe_recv, (last - my_part, owner)
            ).start()

        each_other(send)
        pl.when(my_part > 0)(lambda: send(me))

        @pl.when(my_part == 0)
        def _():
            pltpu.make_async_copy(owed.at[me], owing.at[my_cut], owe_recv).start()

    @pl.when(section == 0)
    def _():
        pass_lists(first_hidden())

    if sections > 2:
        @pl.when((section > 0) & (section < last))
        def _():
            if_slicing(lambda: take_lists(False))
            pass_lists(next_hidden())

    @pl.when(section == last)
    def _():
        if_slicing(lambda: take_lists(True))
        share_parts(next_hidden())

    def done_copy(far):
        mine = last - section
        return remote(
            done_out, done_in.at[mine], done_send.at[far], done_recv.at[mine],
            (far_pipe(far), me),
        )

    def finish(q):
        wait(owing, owe_recv)
        for c in range(CUT):
            for b in range(blocks):
                rows = owing[c, b].astype(jnp.float32)
                for t in range(window // LANE):
                    held[t, pl.ds(b * filled * CUT + c, filled, stride=CUT)] = rows[
                        :filled, t * LANE : (t + 1) * LANE
                    ]
        span = returned.at[:, :, pl.ds(plan.off[q], plan.size[q])]
        wait(span, part_recv)
        lanes = slice(plan.off[q], plan.off[q] + plan.size[q])
        updates = [
            jnp.sum(returned[pl.ds(e * group, group), :, lanes].astype(jnp.float32), axis=0)
            for e in range(experts)
        ]
        for slot in range(slots):
            for t in range(plan.size[q] // LANE):
                tile = plan.off[q] // LANE + t
                rows = held[tile, pl.ds(slot * CUT, CUT)]
                for e in range(experts):
                    same = place[slot] == place[last * experts + e]
                    rows += jnp.where(same, updates[e][:, t * LANE : (t + 1) * LANE], 0.0)
                done_out[slot, :, tile * LANE : (tile + 1) * LANE] = rows.astype(jnp.bfloat16)
        for far in range(1, sections):
            remote(
                done_out.at[:, :, pl.ds(plan.off[q], plan.size[q])],
                done_in.at[q, :, :, pl.ds(plan.off[q], plan.size[q])],
                done_send.at[far], done_recv.at[q], (far_pipe(far), me),
            ).start()

        done_in[q, :, :, lanes] = done_out[:, :, lanes]

    for q in range(parts):
        pl.when(section == last - q)(functools.partial(finish, q))

    for q in range(parts):
        @pl.when(section != last - q)
        def _():
            wait(done_in.at[q, :, :, pl.ds(plan.off[q], plan.size[q])], done_recv.at[q])

    def over_cuts(value):
        count, lanes = value.shape
        summed = jnp.sum(value.reshape(count // CUT, CUT, lanes), axis=1, keepdims=True)
        return jnp.broadcast_to(summed, (count // CUT, CUT, lanes)).reshape(count, lanes)

    height = slots * CUT
    wide = jnp.concatenate(
        [done_in[q][:, :, plan.off[q] : plan.off[q] + plan.size[q]].astype(jnp.float32)
         for q in range(parts)], axis=2,
    ).reshape(height, piece)
    mean = over_cuts(jnp.sum(wide * wide, axis=1, keepdims=True)) * (1.0 / features)
    narrow = wide.astype(jnp.bfloat16)
    feats = probe_ref.shape[0]
    cut_out = lax.rem(lax.broadcasted_iota(jnp.int32, (height, feats), 0), CUT)
    changed = jnp.zeros((height, feats), jnp.float32)
    for c in range(CUT):
        term = lax.dot_general(
            narrow, probe_ref[:, c * piece : (c + 1) * piece], NT,
            preferred_element_type=jnp.float32,
        )
        changed = jnp.where(cut_out == c, term, changed)
    changed = over_cuts(changed) * lax.rsqrt(mean + EPS)
    token_id = lax.broadcasted_iota(jnp.int32, (tokens, feats), 0).astype(jnp.float32)
    result = base
    for slot in range(slots):
        at = place[slot][:1, :feats]
        result = jnp.where(token_id == at, changed[slot * CUT : slot * CUT + 1], result)
    out_ref[...] = result.astype(out_ref.dtype)

    @pl.when(section == 0)
    def _():
        most = arrived.at[pl.ds(0, width - 1)]
        wait(most, row_send)

    @pl.when(section < last)
    def _():
        for _ in range(1):
            whole = pin.at[pl.ds(0, CUT * parts)]
            wait(whole, pin_send)
        if sections > 2:
            @pl.when(section > 0)
            def _():
                if_slicing(lambda: wait(state_out, state_send))

    @pl.when(section == 1)
    def _():
        slices = CUT * parts
        if per == parts:
            wait(xin.at[pl.ds(0, slices - 1)], x_send)
        else:
            pl.when(my_part < parts)(lambda: wait(xin.at[pl.ds(0, slices - 1)], x_send))
            pl.when(my_part >= parts)(lambda: wait(xin.at[pl.ds(0, slices)], x_send))

    @pl.when(section > 0)
    def _():
        if_slicing(lambda: wait(fed.at[pl.ds(0, width - 1)], fed_send))

    @pl.when(section == last)
    def _():
        def owed_left():
            pl.when(my_part == 0)(lambda: wait(owed.at[pl.ds(0, width - 1)], owe_send))
            pl.when(my_part > 0)(lambda: wait(owed, owe_send))

        if_slicing(owed_left)
        for q in range(parts):
            span = partial.at[
                pl.ds(0, width if q else width - 1), :, pl.ds(plan.start[q], plan.size[q])
            ]
            wait(span, part_send.at[q])

    for q in range(parts):
        @pl.when(section == last - q)
        def _():
            for far in range(1, sections):
                wait(done_out.at[:, :, pl.ds(plan.off[q], plan.size[q])], done_send.at[far])


def shards(inputs, router, w_up, w_down, picks, probe):
    sections = lax.axis_size("pipe")
    width = lax.axis_size("expert")
    tokens, features = inputs.shape[1:]
    experts = router.shape[2]
    cap = picks.shape[3]
    hidden_units = w_up.shape[1]
    feats = probe.shape[1]
    piece = features // CUT
    slots = sections * experts
    blocks = -(-slots // BLOCK)
    plan = Plan(sections, width, features)
    window, parts = plan.window, plan.parts
    any_spec = pl.BlockSpec(memory_space=pl.ANY)
    low, wide = jnp.bfloat16, jnp.float32
    state = (slots, cap, window) if sections > 2 else (1, 8, LANE)
    dma = pltpu.SemaphoreType.DMA
    out = pl.pallas_call(
        functools.partial(kernel, sections, width, experts, plan),
        out_shape=jax.ShapeDtypeStruct((tokens, feats), jnp.bfloat16),
        in_specs=[any_spec] * 6,
        out_specs=pl.BlockSpec(memory_space=pltpu.VMEM),
        scratch_shapes=[
            pltpu.VMEM((tokens, features), low),
            pltpu.VMEM((hidden_units + PAD, features), low),
            pltpu.VMEM((hidden_units, features), low),
            pltpu.VMEM((feats, features), low),
            pltpu.VMEM((experts, features), low),
            pltpu.VMEM((sections, experts, cap), jnp.int32),
            pltpu.VMEM((slots, cap, LANE), wide),
            pltpu.VMEM((slots, CUT, LANE), wide),
            pltpu.VMEM((experts, CUT, piece), low),
            pltpu.VMEM((width, CUT, piece), low),
            pltpu.VMEM((piece // LANE, width * CUT, LANE), wide),
            pltpu.VMEM((CUT, cap, piece), low),
            pltpu.VMEM((CUT, blocks, BLOCK, piece), low),
            pltpu.VMEM((width, blocks, BLOCK, window), low),
            pltpu.VMEM((slots, cap, window), wide),
            pltpu.VMEM((width, cap, window), low),
            pltpu.VMEM(state, low),
            pltpu.VMEM(state, low),
            pltpu.VMEM((experts, cap, window), low),
            pltpu.VMEM((width, cap, window), low),
            pltpu.VMEM((width, blocks, BLOCK, window), low),
            pltpu.VMEM((CUT, blocks, BLOCK, window), low),
            pltpu.VMEM((window // LANE, slots * CUT, LANE), wide),
            pltpu.VMEM((width, CUT, piece), low),
            pltpu.VMEM((width, CUT, window), low),
            pltpu.VMEM((slots, CUT, window), low),
            pltpu.VMEM((parts, slots, CUT, window), low),
            dma((6,)), dma((sections,)), dma((sections,)), dma, dma,
            dma, dma, dma, dma, dma, dma,
            dma, dma((width,)), dma, dma,
            dma((parts,)), dma, dma((sections,)), dma((parts,)),
        ],
        compiler_params=pltpu.CompilerParams(collective_id=0, has_side_effects=True),
        name="relay",
    )(inputs[0], jnp.transpose(router[0]), w_up[0], w_down[0], picks[0, 0], probe[0])
    return out[None, None]


def solution(mesh):
    return jax.shard_map(
        shards,
        mesh=mesh,
        in_specs=(
            P(None, "expert", None),
            P("pipe", None, None),
            P("pipe", "expert", None),
            P("pipe", "expert", None),
            P("pipe", None, None, None),
            P("pipe", None, None),
        ),
        out_specs=P("pipe", None, "expert", None),
        check_vma=False,
    )
```

time: 36.8 us -> 36.4 us (0.989)
  the two profiles are of different devices: /device:TPU:3 before, /device:TPU:0 now
where the time goes in v1:
time: 36.4 us; the launch traced here: 36.2 us
  Pallas kernels  34.9 us (96%)
  local copies, waits for them, and re-layouts  1.3 us (4%)
    pallas_call x1, Pallas kernels, shards(): pl.pallas_call(functools.partial(kernel, sections, width, experts, plan),...  34.9 us
    unnamed x1, local copies, waits for them, and re-layouts  1.3 us

profile of v1, /device:TPU:0, one launch (start us, length us, event | category | flops | bytes accessed | tf_op | source)
XLA Modules:
  0.0 36.2 jit_solution(13373223035688246546)
XLA Ops:
  0.0 34.9 %relay.1 = bf16[32,64]{1,0:T(8,128)(2,1)} custom-call(bf16[32,5120]{1,0:T(8,128)(2,1)} %bitcast.12, bf16[2,5120]{1,0:T(2,128)(2,1)} %bitcast.14, bf16[192,5120]{1,0:T(8,128)(2,1)} %bitcast.9, bf16[192,5120]{1,0:T(8,128)(2,1)} %bitcast.10, s32[2,8]{1,0:T(2,128)} %bitcast.15, bf16[64,5120]{1,0:T(8,128)(2,1)} %bitcast.11), custom_call_target="tpu_custom_call" | custom-call | tf_op jit(solution)/shard_map/relay/pallas_call | solution.py:606
  34.9 1.3 %copy.8 = bf16[1,1,32,64]{3,2,1,0:T(8,128)(2,1)} copy(bf16[1,1,32,64]{3,2,1,0:T(8,128)(2,1)} %bitcast.13) | data formatting | bytes 8192

commit v2 on v1

--- a/solution.py
+++ b/solution.py
@@ -11,6 +11,8 @@
 CUT = 8
 PAD = 16
 JOIN = 2
+GROUPS = 2
+GRANT = 24 << 20
 LANE = 128
 BLOCK = 8
 MESH = pl.DeviceIdType.MESH
@@ -38,7 +40,7 @@
     stage, listed, xrows, xin, base_rows, pin, state_out, state_in, sent, fed, owed, owing, held,
     partial, returned, done_out, done_in, load_sem, list_send, list_recv, row_send, row_recv,
     x_send, x_recv, pin_send, pin_recv, state_send, state_recv, fed_send, fed_recv, owe_send,
-    owe_recv, part_send, part_recv, done_send, done_recv,
+    owe_recv, part_send, part_recv, done_send, done_recv, swap_send, swap_recv, self_sem, ready,
 ):
     section = lax.axis_index("pipe")
     me = lax.axis_index("expert")
@@ -83,15 +85,19 @@
     def wait(ref, sem):
         pltpu.make_async_copy(ref, ref, sem).wait()
 
-    def greet(other):
-        for far in range(sections):
+    partners = [jnp.bitwise_xor(me, group * k) for k in range(1, experts)]
+    block = [jnp.bitwise_xor(me, m) for m in reversed(range(1, group))]
+
+    def greet(others):
+        for other in others:
             pl.semaphore_signal(
-                barrier, inc=1, device_id=(far_pipe(far), other), device_id_type=MESH
-            )
-
+                barrier, inc=1, device_id=(section, other), device_id_type=MESH
+            )
+
+    greet(partners)
+    greet(block)
     for far in range(1, sections):
         pl.semaphore_signal(barrier, inc=1, device_id=(far_pipe(far), me), device_id_type=MESH)
-    each_other(greet)
 
     loads = [
         pltpu.make_async_copy(picks_hbm, lists.at[section], load_sem.at[0]),
@@ -150,7 +156,7 @@
     def _():
         picked[...] = select(places).astype(jnp.bfloat16).reshape(experts, CUT, piece)
 
-    pl.semaphore_wait(barrier, sections * width - 1)
+    pl.semaphore_wait(barrier, group - 1 + experts - 1 + sections - 1)
 
     def expert_of(index):
         owner = jnp.int32(0)
@@ -160,12 +166,19 @@
 
     @pl.when(section == 0)
     def _():
-        each_other(
-            lambda other: remote(
-                picked.at[expert_of(other)], arrived.at[me], row_send, row_recv, (section, other)
+        for k in range(1, experts):
+            remote(
+                picked.at[jnp.bitwise_xor(expert, k)], arrived.at[me], swap_send, swap_recv.at[k],
+                (section, partners[k - 1]),
             ).start()
-        )
-        pltpu.make_async_copy(picked.at[expert], arrived.at[me], row_recv).start()
+        for other in block:
+            remote(
+                picked.at[expert], arrived.at[me], row_send, row_recv, (section, other)
+            ).start()
+        pltpu.make_async_copy(picked.at[expert], arrived.at[me], self_sem).start()
+
+    for other in partners:
+        pl.semaphore_signal(ready.at[0], inc=1, device_id=(section, other), device_id_type=MESH)
 
     def list_copy(far):
         return remote(
@@ -175,6 +188,29 @@
 
     for far in range(1, sections):
         list_copy(far).start()
+
+    loads[5].wait()
+    x_all = x_ref[...]
+    raw = lax.dot_general(x_all, probe_ref[...], NT, preferred_element_type=jnp.float32)
+    x_wide = x_all.astype(jnp.float32)
+    square = jnp.sum(x_wide * x_wide, axis=1, keepdims=True)
+    base = raw * lax.rsqrt(square * (1.0 / features) + EPS)
+
+    @pl.when(section == 0)
+    def _():
+        for k in range(1, experts):
+            wait(arrived.at[partners[k - 1]], swap_recv.at[k])
+        for other in block:
+            for partner in partners:
+                remote(
+                    arrived.at[partner], arrived.at[partner], row_send, row_recv, (section, other)
+                ).start()
+
+    pl.semaphore_wait(ready.at[0], experts - 1)
+    for far in range(1, sections):
+        pl.semaphore_signal(
+            ready.at[1], inc=1, device_id=(far_pipe(far), me), device_id_type=MESH
+        )
     for far in range(1, sections):
         list_copy(far).wait()
         note(lax.rem(section + sections - far, sections))
@@ -236,18 +272,12 @@
 
         each_slice(send)
 
-    loads[5].wait()
-    x_all = x_ref[...]
-    raw = lax.dot_general(x_all, probe_ref[...], NT, preferred_element_type=jnp.float32)
-    x_wide = x_all.astype(jnp.float32)
-    square = jnp.sum(x_wide * x_wide, axis=1, keepdims=True)
-    base = raw * lax.rsqrt(square * (1.0 / features) + EPS)
-
     loads[2].wait()
     loads[3].wait()
     up_ref[pl.ds(hidden_units, PAD)] = jnp.zeros((PAD, features), jnp.bfloat16)
     up_ref[pl.ds(hidden_units, experts)] = scorer[...]
     loads[4].wait()
+    pl.semaphore_wait(ready.at[1], sections - 1)
 
     @pl.when(section == 1)
     def _():
@@ -273,7 +303,8 @@
         return (value / (1.0 + jnp.exp(-value)) * gate).astype(jnp.bfloat16)
 
     def first_hidden():
-        wait(arrived, row_recv)
+        wait(arrived.at[me], self_sem)
+        wait(arrived.at[pl.ds(0, (group - 1) * experts)], row_recv)
         wide = arrived[...].astype(jnp.float32).reshape(width * CUT, piece)
         for t in range(piece // LANE):
             stage[t] = wide[:, t * LANE : (t + 1) * LANE]
@@ -296,30 +327,36 @@
 
     def next_hidden():
         pre = jnp.zeros((cap, up_ref.shape[0]), jnp.float32)
-        squares = jnp.zeros((cap, piece), jnp.float32)
-        for step in range(CUT):
-            cut = jnp.bitwise_xor(my_cut, step)
-            for q in range(parts):
-                wait(fed.at[cut * per + q], fed_recv.at[cut * per + q])
+        squares = jnp.zeros((cap, 1), jnp.float32)
+        span = CUT // GROUPS
+        for first in range(0, CUT, span):
+            start = jnp.bitwise_xor(my_cut // span * span, first)
+            for i in range(span):
+                for q in range(parts):
+                    device = (start + i) * per + q
+                    wait(fed.at[device], fed_recv.at[device])
             chunk = jnp.concatenate(
-                [fed[cut * per + q][:, plan.off[q] : plan.off[q] + plan.size[q]]
-                 for q in range(parts)], axis=1,
+                [fed[(start + i) * per + q][:, plan.off[q] : plan.off[q] + plan.size[q]]
+                 for i in range(span) for q in range(parts)], axis=1,
             )
             wide = chunk.astype(jnp.float32)
-            squares += wide * wide
+            squares += jnp.sum(wide * wide, axis=1, keepdims=True)
             pre += lax.dot_general(
-                chunk, up_ref[:, pl.ds(pl.multiple_of(cut * piece, LANE), piece)], NT,
+                chunk, up_ref[:, pl.ds(pl.multiple_of(start * piece, LANE), span * piece)], NT,
                 preferred_element_type=jnp.float32,
             )
-        return hidden_of(pre, jnp.sum(squares, axis=1, keepdims=True))
+        return hidden_of(pre, squares)
 
     def pass_lists(hidden):
+        for c in range(0, CUT, JOIN):
+            block = jnp.dot(
+                hidden, down_ref[:, c * piece : (c + JOIN) * piece],
+                preferred_element_type=jnp.float32,
+            ).astype(jnp.bfloat16)
+            for i in range(JOIN):
+                listed[c + i] = block[:, i * piece : (i + 1) * piece]
+
         def send(step, cut, q, device):
-            if q == 0:
-                listed[cut] = jnp.dot(
-                    hidden, down_ref[:, pl.ds(pl.multiple_of(cut * piece, LANE), piece)],
-                    preferred_element_type=jnp.float32,
-                ).astype(jnp.bfloat16)
             remote(
                 listed.at[cut, :, pl.ds(plan.win[q], window)], pin.at[me], pin_send, pin_recv,
                 (section + 1, device),
@@ -382,6 +419,15 @@
                 wait(state_in, state_recv)
                 base_rows[...] = state_in[...].astype(jnp.float32)
 
+        before = columns[pl.ds((section - 1) * experts, experts)]
+        entries = row_of(before.reshape(experts * cap, before.shape[2])[:, :1])
+
+        def matches(first, count):
+            wide = columns[pl.ds(first, count)]
+            same = wide.reshape(count * cap, wide.shape[2])[:, :1] == entries
+            return jnp.where(same, 1.0, 0.0).astype(jnp.bfloat16)
+
+        own = matches(section * experts, experts)
         wait(pin, pin_recv)
         sums = jnp.concatenate(
             [jnp.sum(pin[pl.ds(e * group, group)].astype(jnp.float32), axis=0)
@@ -389,20 +435,15 @@
         )
         high = sums.astype(jnp.bfloat16)
         low = (sums - high.astype(jnp.float32)).astype(jnp.bfloat16)
-        before = columns[pl.ds((section - 1) * experts, experts)]
-        entries = row_of(before.reshape(experts * cap, before.shape[2])[:, :1])
-
-        def grow(first, count):
-            wide = columns[pl.ds(first, count)]
-            same = wide.reshape(count * cap, wide.shape[2])[:, :1] == entries
-            hot = jnp.where(same, 1.0, 0.0).astype(jnp.bfloat16)
+
+        def grow(hot, first, count):
             added = jnp.dot(hot, high, preferred_element_type=jnp.float32) + jnp.dot(
                 hot, low, preferred_element_type=jnp.float32
             )
             rows = base_rows[pl.ds(first, count)] + added.reshape(count, cap, window)
             return rows.astype(jnp.bfloat16)
 
-        sent[...] = grow(section * experts, experts)
+        sent[...] = grow(own, section * experts, experts)
         each_other(
             lambda other: remote(
                 sent.at[expert_of(other)], fed.at[me], fed_send, fed_recv.at[me], (section, other)
@@ -410,7 +451,7 @@
         )
         pltpu.make_async_copy(sent.at[expert], fed.at[me], fed_recv.at[me]).start()
         for b in range(blocks):
-            rows = grow(b * filled, filled)
+            rows = grow(matches(b * filled, filled), b * filled, filled)
             if sections > 2:
                 state_out[pl.ds(b * filled, filled)] = rows
             owed_block(b, rows.reshape(filled * cap, window))
@@ -540,8 +581,8 @@
 
     @pl.when(section == 0)
     def _():
-        most = arrived.at[pl.ds(0, width - 1)]
-        wait(most, row_send)
+        wait(arrived.at[pl.ds(0, (group - 1) * experts)], row_send)
+        wait(picked.at[pl.ds(0, experts - 1)], swap_send)
 
     @pl.when(section < last)
     def _():
@@ -603,6 +644,9 @@
     low, wide = jnp.bfloat16, jnp.float32
     state = (slots, cap, window) if sections > 2 else (1, 8, LANE)
     dma = pltpu.SemaphoreType.DMA
+    arrays = (
+        inputs[0], jnp.transpose(router[0]), w_up[0], w_down[0], picks[0, 0], probe[0],
+    )
     out = pl.pallas_call(
         functools.partial(kernel, sections, width, experts, plan),
         out_shape=jax.ShapeDtypeStruct((tokens, feats), jnp.bfloat16),
@@ -640,10 +684,13 @@
             dma, dma, dma, dma, dma, dma,
             dma, dma((width,)), dma, dma,
             dma((parts,)), dma, dma((sections,)), dma((parts,)),
+            dma, dma((experts,)), dma, pltpu.SemaphoreType.REGULAR((2,)),
         ],
-        compiler_params=pltpu.CompilerParams(collective_id=0, has_side_effects=True),
+        compiler_params=pltpu.CompilerParams(
+            collective_id=0, has_side_effects=True, vmem_limit_bytes=GRANT
+        ),
         name="relay",
-    )(inputs[0], jnp.transpose(router[0]), w_up[0], w_down[0], picks[0, 0], probe[0])
+    )(*[pltpu.with_memory_space_constraint(array, pltpu.HBM) for array in arrays])
     return out[None, None]
 
 

time: 36.4 us -> 34.8 us (0.956)
  Pallas kernels: 34.9 us -> 34 us
  local copies, waits for them, and re-layouts: 1.3 us -> 0.6 us
    pallas_call x1, Pallas kernels: 34.9 us -> 34 us  [shards(): pl.pallas_call(functools.partial(kernel, sections, width, experts, plan),...]
    unnamed x1, local copies, waits for them, and re-layouts: 1.3 us -> 0.6 us
where the time goes in v2:
time: 34.8 us; the launch traced here: 34.6 us
  Pallas kernels  34 us (98%)
  local copies, waits for them, and re-layouts  0.6 us (2%)
    pallas_call x1, Pallas kernels, shards(): pl.pallas_call(functools.partial(kernel, sections, width, experts, plan),...  34 us

profile of v2, /device:TPU:0, one launch (start us, length us, event | category | flops | bytes accessed | tf_op | source)
XLA Modules:
  0.0 34.6 jit_solution(8751281522979348088)
XLA Ops:
  0.0 34.0 %relay.1 = bf16[32,64]{1,0:T(8,128)(2,1)S(1)} custom-call(bf16[32,5120]{1,0:T(8,128)(2,1)} %bitcast.13, bf16[2,5120]{1,0:T(2,128)(2,1)} %bitcast.14, bf16[192,5120]{1,0:T(8,128)(2,1)} %bitcast.10, bf16[192,5120]{1,0:T(8,128)(2,1)} %bitcast.11, s32[2,8]{1,0:T(2,128)} %bitcast.15, bf16[64,5120]{1,0:T(8,128)(2,1)} %bitcast.12), custom_call_target="tpu_custom_call" | custom-call | tf_op jit(solution)/shard_map/relay/pallas_call | solution.py:650
  34.0 0.6 %copy.8 = bf16[1,1,32,64]{3,2,1,0:T(8,128)(2,1)} copy(bf16[1,1,32,64]{3,2,1,0:T(8,128)(2,1)S(1)} %bitcast.9) | data formatting | bytes 8192

commit v3 on v2

--- a/solution.py
+++ b/solution.py
@@ -335,6 +335,8 @@
                 for q in range(parts):
                     device = (start + i) * per + q
                     wait(fed.at[device], fed_recv.at[device])
+            if first == 0:
+                pl.when(section == last)(lambda: if_slicing(owe))
             chunk = jnp.concatenate(
                 [fed[(start + i) * per + q][:, plan.off[q] : plan.off[q] + plan.size[q]]
                  for i in range(span) for q in range(parts)], axis=1,
@@ -348,15 +350,18 @@
         return hidden_of(pre, squares)
 
     def pass_lists(hidden):
-        for c in range(0, CUT, JOIN):
-            block = jnp.dot(
-                hidden, down_ref[:, c * piece : (c + JOIN) * piece],
-                preferred_element_type=jnp.float32,
-            ).astype(jnp.bfloat16)
-            for i in range(JOIN):
-                listed[c + i] = block[:, i * piece : (i + 1) * piece]
+        span = CUT // GROUPS
 
         def send(step, cut, q, device):
+            if step % span == span - 1 and q == 0:
+                first = cut // span * span
+                block = jnp.dot(
+                    hidden,
+                    down_ref[:, pl.ds(pl.multiple_of(first * piece, LANE), span * piece)],
+                    preferred_element_type=jnp.float32,
+                ).astype(jnp.bfloat16)
+                for i in range(span):
+                    listed[first + i] = block[:, i * piece : (i + 1) * piece]
             remote(
                 listed.at[cut, :, pl.ds(plan.win[q], window)], pin.at[me], pin_send, pin_recv,
                 (section + 1, device),
@@ -374,20 +379,6 @@
             jnp.where(hot, 1.0, 0.0).astype(jnp.bfloat16), hidden,
             preferred_element_type=jnp.float32,
         ).astype(jnp.bfloat16)
-        for c in range(0, CUT, JOIN):
-            block = jnp.dot(
-                hidden, down_ref[:, c * piece : (c + JOIN) * piece],
-                preferred_element_type=jnp.float32,
-            )
-            for i in range(JOIN):
-                for t in range(piece // LANE):
-                    at = i * piece + t * LANE
-                    stage[t, pl.ds(c + i, width, stride=CUT)] = block[:, at : at + LANE]
-        for t in range(piece // LANE):
-            partial[:, :, t * LANE : (t + 1) * LANE] = (
-                stage[t].reshape(width, CUT, LANE).astype(jnp.bfloat16)
-            )
-
         def refs(owner, q):
             return (
                 partial.at[owner, :, pl.ds(plan.start[q], plan.size[q])],
@@ -398,14 +389,29 @@
             src, dst = refs(owner, q)
             remote(src, dst, part_send.at[q], part_recv, (section - q, owner)).start()
 
-        for q in reversed(range(1, parts)):
-            give(me, q)
-
-        def give_all(owner):
-            for q in reversed(range(parts)):
-                give(owner, q)
-
-        each_other(give_all)
+        for q in reversed(range(parts)):
+            first, count, size = plan.start[q] // LANE, plan.size[q] // LANE, plan.size[q]
+            for c in range(0, CUT, JOIN):
+                columns_of = [
+                    down_ref[:, pl.ds((c + i) * piece + plan.start[q], size)] for i in range(JOIN)
+                ]
+                product = jnp.dot(
+                    hidden, jnp.concatenate(columns_of, axis=1),
+                    preferred_element_type=jnp.float32,
+                )
+                for i in range(JOIN):
+                    for t in range(count):
+                        at = i * size + t * LANE
+                        stage[first + t, pl.ds(c + i, width, stride=CUT)] = product[
+                            :, at : at + LANE
+                        ]
+            for t in range(first, first + count):
+                partial[:, :, t * LANE : (t + 1) * LANE] = (
+                    stage[t].reshape(width, CUT, LANE).astype(jnp.bfloat16)
+                )
+            each_other(functools.partial(give, q=q))
+            if q:
+                give(me, q)
         src, dst = refs(me, 0)
         pltpu.make_async_copy(src, dst, part_recv).start()
 
@@ -457,7 +463,6 @@
             owed_block(b, rows.reshape(filled * cap, window))
         if sections > 2:
             pl.when(section < last)(lambda: state_copy().start())
-        pl.when(section == last)(owe)
 
     def owed_block(b, rows):
         @pl.when(section == last)

time: 34.8 us -> 34.1 us (0.980)
  Pallas kernels: 34 us -> 33.3 us
    pallas_call x1, Pallas kernels: 34 us -> 33.3 us  [shards(): pl.pallas_call(functools.partial(kernel, sections, width, experts, plan),...]
where the time goes in v3:
time: 34.1 us; the launch traced here: 34 us
  Pallas kernels  33.3 us (98%)
  local copies, waits for them, and re-layouts  0.6 us (2%)
    pallas_call x1, Pallas kernels, shards(): pl.pallas_call(functools.partial(kernel, sections, width, experts, plan),...  33.3 us

profile of v3, /device:TPU:0, one launch (start us, length us, event | category | flops | bytes accessed | tf_op | source)
XLA Modules:
  0.0 34.0 jit_solution(8524421119996121516)
XLA Ops:
  0.0 33.3 %relay.1 = bf16[32,64]{1,0:T(8,128)(2,1)S(1)} custom-call(bf16[32,5120]{1,0:T(8,128)(2,1)} %bitcast.13, bf16[2,5120]{1,0:T(2,128)(2,1)} %bitcast.14, bf16[192,5120]{1,0:T(8,128)(2,1)} %bitcast.10, bf16[192,5120]{1,0:T(8,128)(2,1)} %bitcast.11, s32[2,8]{1,0:T(2,128)} %bitcast.15, bf16[64,5120]{1,0:T(8,128)(2,1)} %bitcast.12), custom_call_target="tpu_custom_call" | custom-call | tf_op jit(solution)/shard_map/relay/pallas_call | solution.py:655
  33.4 0.6 %copy.8 = bf16[1,1,32,64]{3,2,1,0:T(8,128)(2,1)} copy(bf16[1,1,32,64]{3,2,1,0:T(8,128)(2,1)S(1)} %bitcast.9) | data formatting | bytes 8192
